TPU v7x, 32 devices: a whole 2x2x4 slice. The times are simulated.
32 devices in a mesh: row: 8 (over z, x), col: 4 (over y, core).
Axes of the slice: x: 2, y: 2, z: 4, core: 2. Of those that a mesh axis runs over, the one named last changes fastest.
Arguments:
- vectors: float32 [8192, 1024], P(('row', 'col')), may hold values from -6 to 6
- rotation: float32 [1024, 1024], P(None, 'col'), may hold values from -0.1875 to 0.1875
- blocks: bfloat16 [64, 16, 128, 128], P('row'), may hold values from -0.0625 to 0.0625
- cols: int32 [64, 16], P('row'), may hold values from 0 to 15, as said below
- lists: int32 [8, 2, 4], P('row'), may hold values from 0 to 7, as said below
- counts: int32 [8], P('row'), may hold values from 4 to 8, as said below
Outputs:
- filtered: float32 [1024, 8192], P('col', 'row')
Inputs may be any that keep to these rules, and one draw needn't show every extreme that they name: `counts`: at least one group uses all 8 slots. Every entry of lists[r] is below counts[r], and lists[r, j, 0] = counts[r] - 1; entries may repeat. cols[t, 0] = 4 + t % 8, the block row itself; on valid block rows of group r every slot between 4 and 15 that names an own block row is below 4 + counts[r].
All inputs are finite; a program needn't handle non-finite values.
Results may differ from a plain program's by a relative error of at most 0.0065.
Values may be sent and summed in bfloat16 or wider, within the bound.
No kernel may reach another device: no remote copies, remote signals or barrier semaphores. Data moves between devices by JAX's collectives and lax.ppermute only.
A program may use at most 64 MiB of HBM per device.

v0:
```python
import jax
import jax.numpy as jnp
from jax import lax
from jax.sharding import PartitionSpec as P

STEPS = 10


def passed_along(x, axis, by):
    length = lax.axis_size(axis)
    pairs = [(i, i + by) for i in range(length) if 0 <= i + by < length]
    return lax.ppermute(x, axis, pairs)


def apply_blocks(field, blocks, cols, lists, valid):
    lowered = field.astype(jnp.bfloat16)
    up_rows = lowered[:, lists[0, 0], :]
    down_rows = lowered[:, lists[0, 1], :]
    from_prev = passed_along(up_rows, "row", 1)
    from_next = passed_along(down_rows, "row", -1)
    source = jnp.concatenate([from_prev, lowered, from_next], axis=1)
    picked = source[:, cols, :]
    result = jnp.einsum("cbkj,bkij->cbi", picked, blocks, preferred_element_type=jnp.float32)
    return result * valid[None, :, None]


def body(vectors, rotation, blocks, cols, lists, counts):
    cap = blocks.shape[0]
    width = blocks.shape[2]
    panel = lax.dot_general(
        rotation,
        lax.all_gather(vectors, "col", axis=0, tiled=True),
        (((0,), (1,)), ((), ())),
        precision=lax.Precision.HIGHEST,
        preferred_element_type=jnp.float32,
    )
    panel_cols = panel.shape[0]
    valid = (jnp.arange(cap, dtype=jnp.int32) < counts[0]).astype(jnp.float32)
    previous = panel.reshape(panel_cols, cap, width) * valid[None, :, None]
    current = apply_blocks(previous, blocks, cols, lists, valid)

    def advance(index, carry):
        older, newer = carry
        return (newer, 2.0 * apply_blocks(newer, blocks, cols, lists, valid) - older)

    previous, current = lax.fori_loop(0, STEPS - 1, advance, (previous, current))
    return current.reshape(panel_cols, cap * width)


def solution(mesh):
    return jax.shard_map(
        body,
        mesh=mesh,
        in_specs=(
            P(("row", "col"), None),
            P(None, "col"),
            P("row", None, None, None),
            P("row", None),
            P("row", None, None),
            P("row"),
        ),
        out_specs=P("col", "row"),
        check_vma=False,
    )
```

profile of v0, /device:TPU:0, one launch (start us, length us, event | category | flops | bytes accessed | tf_op | source)
XLA Modules:
  0.0 394.8 jit_solution(11017136291069954017)
XLA Ops:
  8.7 37.4 %all-gather.2.cloned.1.call-done = f32[1024,1024]{1,0:T(8,128)} async-done(((f32[256,1024]{1,0:T(8,128)}), f32[1024,1024]{1,0:T(8,128)}) %all-gather.2.cloned.1.call-update) | async-done | bytes 4194320 | tf_op jit(solution)/shard_map/all_gather | solution.py:32
  46.1 8.7 %convolution_bitcast_fusion.2 = f32[32,8,8,128]{3,2,1,0:T(8,128)S(1)} fusion(f32[1024,256]{1,0:T(8,128)S(1)} %copy-done, f32[1024,1024]{1,0:T(8,128)} %all-gather.2.cloned.1.call-done), kind=kOutput, calls=%fused_computation.25 | convolution fusion | flops 3221225472 | bytes 6291456 | tf_op jit(solution)/shard_map/dot_general | solution.py:30
  62.1 9.5 %collective-permute-done.2 = bf16[256,4,128]{2,0,1:T(8,128)(2,1)S(1)} collective-permute-done((bf16[256,4,128]{2,0,1:T(8,128)(2,1)S(1)}, bf16[256,4,128]{2,0,1:T(8,128)(2,1)S(1)}, u32[]{:S(2)}, u32[]{:S(2)}) %collective-permute-start.2) | collective-permute-done | bytes 262176 | tf_op jit(solution)/shard_map/ppermute | solution.py:12
  71.7 6.6 %gather_fusion.5 = bf16[128,256,128]{2,1,0:T(8,128)(2,1)} fusion(bf16[256,16,128]{2,0,1:T(8,128)(2,1)S(1)} %pad_maximum_fusion.1, s32[1024]{0:T(1024)S(1)} %pad_clamp_fusion.3), kind=kCustom, calls=%fused_computation.5 | custom fusion | bytes 16777728 | tf_op jit(solution)/shard_map/gather | solution.py:22
  78.3 6.9 %fusion.9 = f32[256,8,128]{2,0,1:T(8,128)S(1)} fusion(bf16[256,8,16,128]{3,0,2,1:T(8,128)(2,1)} %bitcast.93, bf16[8,16,128,128]{3,2,1,0:T(8,128)(2,1)} %param.10, f32[8]{0:T(128)S(1)} %compare_convert_fusion.1), kind=kOutput, calls=%fused_computation.24 | convolution fusion | flops 1074003968 | bytes 13631520 | tf_op jit(solution)/shard_map/cbkj,bkij->cbi/dot_general | solution.py:23
  85.2 301.6 %while.13 = (s32[]{:T(128)}, f32[256,8,128]{2,0,1:T(8,128)}, f32[256,8,128]{2,0,1:T(8,128)S(1)}, s32[1,2,4]{2,1,0:T(2,128)S(1)}, s32[8,16]{1,0:T(8,128)S(1)}, /*...) while((s32[]{:T(128)}, f32[256,8,128]{2,0,1:T(8,128)}, f32[256,8,128]{2,0,1:T(8,128)S(1)}, ...), condition=%wide.region_1.0_spmd.clone, body=%wide.region_0.0_spmd.clone.sunk | while | flops 1075842432 | bytes 44580228 | solution.py:46
  96.2 6.1 %collective-permute-done.1 = bf16[256,4,128]{2,0,1:T(8,128)(2,1)} collective-permute-done((bf16[256,4,128]{2,0,1:T(8,128)(2,1)S(1)}, bf16[256,4,128]{2,0,1:T(8,128)(2,1)}, u32[]{:S(2)}, u32[]{:S(2)}) %collective-permute-start.1) | collective-permute-done | bytes 262176 | tf_op jit(solution)/shard_map/while/body/eval_jaxpr/ppermute | solution.py:12
  103.6 6.6 %gather_fusion.2 = bf16[128,256,128]{2,1,0:T(8,128)(2,1)} fusion(bf16[256,16,128]{2,0,1:T(8,128)(2,1)S(1)} %pad_maximum_fusion.3, s32[1024]{0:T(1024)S(1)} %pad_clamp_fusion.9), kind=kCustom, calls=%fused_computation.2.clone.clone.1 | custom fusion | bytes 16777728 | tf_op jit(solution)/shard_map/while/body/eval_jaxpr/gather | solution.py:22
  110.2 7.2 %fusion.27 = f32[256,8,128]{2,0,1:T(8,128)S(1)} fusion(f32[256,8,128]{2,0,1:T(8,128)} %get-tuple-element.144, bf16[256,8,16,128]{3,0,2,1:T(8,128)(2,1)} %bitcast.92, bf16[8,16,128,128]{3,2,1,0:T(8,128)(2,1)} %get-tuple-element.156, f32[8]{0:T(128)S(1)} %compare_convert_fusion.3), kind=kOutput, calls=%fused_computation.11.clone.1 | convolution fusion | flops 1074528256 | bytes 14680096 | tf_op jit(solution)/shard_map/while/body/eval_jaxpr/cbkj,bkij->cbi/dot_general | solution.py:23
  121.1 5.8 %collective-permute-start.1 = (bf16[256,4,128]{2,0,1:T(8,128)(2,1)S(1)}, bf16[256,4,128]{2,0,1:T(8,128)(2,1)}, u32[]{:S(2)}, u32[]{:S(2)}) collective-permute-start(bf16[256,4,128]{2,0,1:T(8,128)(2,1)S(1)} %bitcast.95), channel_id=1, source_target_pairs={{0,4},{4,8},{8,12},{12,16},{16,20},{20,24},{24,28},{1,5},{5,9},{9,... | collective-permute-start | bytes 786440 | tf_op jit(solution)/shard_map/while/body/eval_jaxpr/ppermute | solution.py:12
  137.1 6.6 %gather_fusion.2 = bf16[128,256,128]{2,1,0:T(8,128)(2,1)} fusion(bf16[256,16,128]{2,0,1:T(8,128)(2,1)S(1)} %pad_maximum_fusion.3, s32[1024]{0:T(1024)S(1)} %pad_clamp_fusion.9), kind=kCustom, calls=%fused_computation.2.clone.clone.1 | custom fusion | bytes 16777728 | tf_op jit(solution)/shard_map/while/body/eval_jaxpr/gather | solution.py:22
  143.7 7.2 %fusion.27 = f32[256,8,128]{2,0,1:T(8,128)S(1)} fusion(f32[256,8,128]{2,0,1:T(8,128)} %get-tuple-element.144, bf16[256,8,16,128]{3,0,2,1:T(8,128)(2,1)} %bitcast.92, bf16[8,16,128,128]{3,2,1,0:T(8,128)(2,1)} %get-tuple-element.156, f32[8]{0:T(128)S(1)} %compare_convert_fusion.3), kind=kOutput, calls=%fused_computation.11.clone.1 | convolution fusion | flops 1074528256 | bytes 14680096 | tf_op jit(solution)/shard_map/while/body/eval_jaxpr/cbkj,bkij->cbi/dot_general | solution.py:23
  154.6 5.8 %collective-permute-start.1 = (bf16[256,4,128]{2,0,1:T(8,128)(2,1)S(1)}, bf16[256,4,128]{2,0,1:T(8,128)(2,1)}, u32[]{:S(2)}, u32[]{:S(2)}) collective-permute-start(bf16[256,4,128]{2,0,1:T(8,128)(2,1)S(1)} %bitcast.95), channel_id=1, source_target_pairs={{0,4},{4,8},{8,12},{12,16},{16,20},{20,24},{24,28},{1,5},{5,9},{9,... | collective-permute-start | bytes 786440 | tf_op jit(solution)/shard_map/while/body/eval_jaxpr/ppermute | solution.py:12
  170.7 6.6 %gather_fusion.2 = bf16[128,256,128]{2,1,0:T(8,128)(2,1)} fusion(bf16[256,16,128]{2,0,1:T(8,128)(2,1)S(1)} %pad_maximum_fusion.3, s32[1024]{0:T(1024)S(1)} %pad_clamp_fusion.9), kind=kCustom, calls=%fused_computation.2.clone.clone.1 | custom fusion | bytes 16777728 | tf_op jit(solution)/shard_map/while/body/eval_jaxpr/gather | solution.py:22
  177.2 7.2 %fusion.27 = f32[256,8,128]{2,0,1:T(8,128)S(1)} fusion(f32[256,8,128]{2,0,1:T(8,128)} %get-tuple-element.144, bf16[256,8,16,128]{3,0,2,1:T(8,128)(2,1)} %bitcast.92, bf16[8,16,128,128]{3,2,1,0:T(8,128)(2,1)} %get-tuple-element.156, f32[8]{0:T(128)S(1)} %compare_convert_fusion.3), kind=kOutput, calls=%fused_computation.11.clone.1 | convolution fusion | flops 1074528256 | bytes 14680096 | tf_op jit(solution)/shard_map/while/body/eval_jaxpr/cbkj,bkij->cbi/dot_general | solution.py:23
  188.2 5.8 %collective-permute-start.1 = (bf16[256,4,128]{2,0,1:T(8,128)(2,1)S(1)}, bf16[256,4,128]{2,0,1:T(8,128)(2,1)}, u32[]{:S(2)}, u32[]{:S(2)}) collective-permute-start(bf16[256,4,128]{2,0,1:T(8,128)(2,1)S(1)} %bitcast.95), channel_id=1, source_target_pairs={{0,4},{4,8},{8,12},{12,16},{16,20},{20,24},{24,28},{1,5},{5,9},{9,... | collective-permute-start | bytes 786440 | tf_op jit(solution)/shard_map/while/body/eval_jaxpr/ppermute | solution.py:12
  204.2 6.6 %gather_fusion.2 = bf16[128,256,128]{2,1,0:T(8,128)(2,1)} fusion(bf16[256,16,128]{2,0,1:T(8,128)(2,1)S(1)} %pad_maximum_fusion.3, s32[1024]{0:T(1024)S(1)} %pad_clamp_fusion.9), kind=kCustom, calls=%fused_computation.2.clone.clone.1 | custom fusion | bytes 16777728 | tf_op jit(solution)/shard_map/while/body/eval_jaxpr/gather | solution.py:22
  210.8 7.2 %fusion.27 = f32[256,8,128]{2,0,1:T(8,128)S(1)} fusion(f32[256,8,128]{2,0,1:T(8,128)} %get-tuple-element.144, bf16[256,8,16,128]{3,0,2,1:T(8,128)(2,1)} %bitcast.92, bf16[8,16,128,128]{3,2,1,0:T(8,128)(2,1)} %get-tuple-element.156, f32[8]{0:T(128)S(1)} %compare_convert_fusion.3), kind=kOutput, calls=%fused_computation.11.clone.1 | convolution fusion | flops 1074528256 | bytes 14680096 | tf_op jit(solution)/shard_map/while/body/eval_jaxpr/cbkj,bkij->cbi/dot_general | solution.py:23
  221.7 5.8 %collective-permute-start.1 = (bf16[256,4,128]{2,0,1:T(8,128)(2,1)S(1)}, bf16[256,4,128]{2,0,1:T(8,128)(2,1)}, u32[]{:S(2)}, u32[]{:S(2)}) collective-permute-start(bf16[256,4,128]{2,0,1:T(8,128)(2,1)S(1)} %bitcast.95), channel_id=1, source_target_pairs={{0,4},{4,8},{8,12},{12,16},{16,20},{20,24},{24,28},{1,5},{5,9},{9,... | collective-permute-start | bytes 786440 | tf_op jit(solution)/shard_map/while/body/eval_jaxpr/ppermute | solution.py:12
  237.8 6.6 %gather_fusion.2 = bf16[128,256,128]{2,1,0:T(8,128)(2,1)} fusion(bf16[256,16,128]{2,0,1:T(8,128)(2,1)S(1)} %pad_maximum_fusion.3, s32[1024]{0:T(1024)S(1)} %pad_clamp_fusion.9), kind=kCustom, calls=%fused_computation.2.clone.clone.1 | custom fusion | bytes 16777728 | tf_op jit(solution)/shard_map/while/body/eval_jaxpr/gather | solution.py:22
  244.3 7.2 %fusion.27 = f32[256,8,128]{2,0,1:T(8,128)S(1)} fusion(f32[256,8,128]{2,0,1:T(8,128)} %get-tuple-element.144, bf16[256,8,16,128]{3,0,2,1:T(8,128)(2,1)} %bitcast.92, bf16[8,16,128,128]{3,2,1,0:T(8,128)(2,1)} %get-tuple-element.156, f32[8]{0:T(128)S(1)} %compare_convert_fusion.3), kind=kOutput, calls=%fused_computation.11.clone.1 | convolution fusion | flops 1074528256 | bytes 14680096 | tf_op jit(solution)/shard_map/while/body/eval_jaxpr/cbkj,bkij->cbi/dot_general | solution.py:23
  255.3 5.8 %collective-permute-start.1 = (bf16[256,4,128]{2,0,1:T(8,128)(2,1)S(1)}, bf16[256,4,128]{2,0,1:T(8,128)(2,1)}, u32[]{:S(2)}, u32[]{:S(2)}) collective-permute-start(bf16[256,4,128]{2,0,1:T(8,128)(2,1)S(1)} %bitcast.95), channel_id=1, source_target_pairs={{0,4},{4,8},{8,12},{12,16},{16,20},{20,24},{24,28},{1,5},{5,9},{9,... | collective-permute-start | bytes 786440 | tf_op jit(solution)/shard_map/while/body/eval_jaxpr/ppermute | solution.py:12
  271.3 6.6 %gather_fusion.2 = bf16[128,256,128]{2,1,0:T(8,128)(2,1)} fusion(bf16[256,16,128]{2,0,1:T(8,128)(2,1)S(1)} %pad_maximum_fusion.3, s32[1024]{0:T(1024)S(1)} %pad_clamp_fusion.9), kind=kCustom, calls=%fused_computation.2.clone.clone.1 | custom fusion | bytes 16777728 | tf_op jit(solution)/shard_map/while/body/eval_jaxpr/gather | solution.py:22
  277.9 7.2 %fusion.27 = f32[256,8,128]{2,0,1:T(8,128)S(1)} fusion(f32[256,8,128]{2,0,1:T(8,128)} %get-tuple-element.144, bf16[256,8,16,128]{3,0,2,1:T(8,128)(2,1)} %bitcast.92, bf16[8,16,128,128]{3,2,1,0:T(8,128)(2,1)} %get-tuple-element.156, f32[8]{0:T(128)S(1)} %compare_convert_fusion.3), kind=kOutput, calls=%fused_computation.11.clone.1 | convolution fusion | flops 1074528256 | bytes 14680096 | tf_op jit(solution)/shard_map/while/body/eval_jaxpr/cbkj,bkij->cbi/dot_general | solution.py:23
  288.8 5.8 %collective-permute-start.1 = (bf16[256,4,128]{2,0,1:T(8,128)(2,1)S(1)}, bf16[256,4,128]{2,0,1:T(8,128)(2,1)}, u32[]{:S(2)}, u32[]{:S(2)}) collective-permute-start(bf16[256,4,128]{2,0,1:T(8,128)(2,1)S(1)} %bitcast.95), channel_id=1, source_target_pairs={{0,4},{4,8},{8,12},{12,16},{16,20},{20,24},{24,28},{1,5},{5,9},{9,... | collective-permute-start | bytes 786440 | tf_op jit(solution)/shard_map/while/body/eval_jaxpr/ppermute | solution.py:12
  304.9 6.6 %gather_fusion.2 = bf16[128,256,128]{2,1,0:T(8,128)(2,1)} fusion(bf16[256,16,128]{2,0,1:T(8,128)(2,1)S(1)} %pad_maximum_fusion.3, s32[1024]{0:T(1024)S(1)} %pad_clamp_fusion.9), kind=kCustom, calls=%fused_computation.2.clone.clone.1 | custom fusion | bytes 16777728 | tf_op jit(solution)/shard_map/while/body/eval_jaxpr/gather | solution.py:22
  311.5 7.2 %fusion.27 = f32[256,8,128]{2,0,1:T(8,128)S(1)} fusion(f32[256,8,128]{2,0,1:T(8,128)} %get-tuple-element.144, bf16[256,8,16,128]{3,0,2,1:T(8,128)(2,1)} %bitcast.92, bf16[8,16,128,128]{3,2,1,0:T(8,128)(2,1)} %get-tuple-element.156, f32[8]{0:T(128)S(1)} %compare_convert_fusion.3), kind=kOutput, calls=%fused_computation.11.clone.1 | convolution fusion | flops 1074528256 | bytes 14680096 | tf_op jit(solution)/shard_map/while/body/eval_jaxpr/cbkj,bkij->cbi/dot_general | solution.py:23
  322.4 5.8 %collective-permute-start.1 = (bf16[256,4,128]{2,0,1:T(8,128)(2,1)S(1)}, bf16[256,4,128]{2,0,1:T(8,128)(2,1)}, u32[]{:S(2)}, u32[]{:S(2)}) collective-permute-start(bf16[256,4,128]{2,0,1:T(8,128)(2,1)S(1)} %bitcast.95), channel_id=1, source_target_pairs={{0,4},{4,8},{8,12},{12,16},{16,20},{20,24},{24,28},{1,5},{5,9},{9,... | collective-permute-start | bytes 786440 | tf_op jit(solution)/shard_map/while/body/eval_jaxpr/ppermute | solution.py:12
  338.4 6.6 %gather_fusion.2 = bf16[128,256,128]{2,1,0:T(8,128)(2,1)} fusion(bf16[256,16,128]{2,0,1:T(8,128)(2,1)S(1)} %pad_maximum_fusion.3, s32[1024]{0:T(1024)S(1)} %pad_clamp_fusion.9), kind=kCustom, calls=%fused_computation.2.clone.clone.1 | custom fusion | bytes 16777728 | tf_op jit(solution)/shard_map/while/body/eval_jaxpr/gather | solution.py:22
  345.0 7.2 %fusion.27 = f32[256,8,128]{2,0,1:T(8,128)S(1)} fusion(f32[256,8,128]{2,0,1:T(8,128)} %get-tuple-element.144, bf16[256,8,16,128]{3,0,2,1:T(8,128)(2,1)} %bitcast.92, bf16[8,16,128,128]{3,2,1,0:T(8,128)(2,1)} %get-tuple-element.156, f32[8]{0:T(128)S(1)} %compare_convert_fusion.3), kind=kOutput, calls=%fused_computation.11.clone.1 | convolution fusion | flops 1074528256 | bytes 14680096 | tf_op jit(solution)/shard_map/while/body/eval_jaxpr/cbkj,bkij->cbi/dot_general | solution.py:23
  372.0 6.6 %gather_fusion.2 = bf16[128,256,128]{2,1,0:T(8,128)(2,1)} fusion(bf16[256,16,128]{2,0,1:T(8,128)(2,1)S(1)} %pad_maximum_fusion.3, s32[1024]{0:T(1024)S(1)} %pad_clamp_fusion.9), kind=kCustom, calls=%fused_computation.2.clone.clone.1 | custom fusion | bytes 16777728 | tf_op jit(solution)/shard_map/while/body/eval_jaxpr/gather | solution.py:22
  378.6 7.2 %fusion.27 = f32[256,8,128]{2,0,1:T(8,128)S(1)} fusion(f32[256,8,128]{2,0,1:T(8,128)} %get-tuple-element.144, bf16[256,8,16,128]{3,0,2,1:T(8,128)(2,1)} %bitcast.92, bf16[8,16,128,128]{3,2,1,0:T(8,128)(2,1)} %get-tuple-element.156, f32[8]{0:T(128)S(1)} %compare_convert_fusion.3), kind=kOutput, calls=%fused_computation.11.clone.1 | convolution fusion | flops 1074528256 | bytes 14680096 | tf_op jit(solution)/shard_map/while/body/eval_jaxpr/cbkj,bkij->cbi/dot_general | solution.py:23
  (176 shorter events, 139.6 us)
Async XLA Ops:
  6.5 39.6 %copy-start = (f32[1024,256]{1,0:T(8,128)S(1)}, f32[1024,256]{1,0:T(8,128)}, u32[]{:S(2)}) copy-start(f32[1024,256]{1,0:T(8,128)} %param.9) | copy-start | bytes 3145732
  6.5 55.4 %copy-start.2 = (s32[8,16]{1,0:T(8,128)S(1)}, s32[8,16]{1,0:T(8,128)}, u32[]{:S(2)}) copy-start(s32[8,16]{1,0:T(8,128)} %param.11) | copy-start | bytes 1540
  6.5 39.6 %all-gather.2.cloned.1.call-start = ((), (), s32[]{:S(2)}) async-start(), calls=%async_computation | async-start | bytes 5242880 | tf_op jit(solution)/shard_map/all_gather | solution.py:32
  56.7 14.9 %collective-permute-start.2 = (bf16[256,4,128]{2,0,1:T(8,128)(2,1)S(1)}, bf16[256,4,128]{2,0,1:T(8,128)(2,1)S(1)}, u32[]{:S(2)}, u32[]{:S(2)}) collective-permute-start(bf16[256,4,128]{2,0,1:T(8,128)(2,1)S(1)} %bitcast.96), channel_id=1, source_target_pairs={{0,4},{4,8},{8,12},{12,16},{16,20},{20,24},{24,28},{1,5},{5,9},{9,... | collective-permute-start | bytes 786440 | tf_op jit(solution)/shard_map/ppermute | solution.py:12
  60.7 10.9 %collective-permute-start.3 = (bf16[256,4,128]{2,0,1:T(8,128)(2,1)S(1)}, bf16[256,4,128]{2,0,1:T(8,128)(2,1)S(1)}, u32[]{:S(2)}, u32[]{:S(2)}) collective-permute-start(bf16[256,4,128]{2,0,1:T(8,128)(2,1)S(1)} %bitcast.97), channel_id=1, source_target_pairs={{4,0},{8,4},{12,8},{16,12},{20,16},{24,20},{28,24},{5,1},{9,5},{13... | collective-permute-start | bytes 786440 | tf_op jit(solution)/shard_map/ppermute | solution.py:12
  85.3 10.9 %copy-start.1 = (bf16[256,8,128]{2,0,1:T(8,128)(2,1)}, bf16[256,8,128]{2,0,1:T(8,128)(2,1)S(1)}, u32[]{:S(2)}) copy-start(bf16[256,8,128]{2,0,1:T(8,128)(2,1)S(1)} %convert_element_type.26) | copy-start | bytes 1572868 | tf_op jit(solution)/shard_map/while
  86.0 10.2 %collective-permute-start = (bf16[256,4,128]{2,0,1:T(8,128)(2,1)S(1)}, bf16[256,4,128]{2,0,1:T(8,128)(2,1)S(1)}, u32[]{:S(2)}, u32[]{:S(2)}) collective-permute-start(bf16[256,4,128]{2,0,1:T(8,128)(2,1)S(1)} %bitcast.94), channel_id=1, source_target_pairs={{4,0},{8,4},{12,8},{16,12},{20,16},{24,20},{28,24},{5,1},{9,5},{13... | collective-permute-start | bytes 786440 | tf_op jit(solution)/shard_map/while/body/eval_jaxpr/ppermute | solution.py:12
  87.9 14.5 %collective-permute-start.1 = (bf16[256,4,128]{2,0,1:T(8,128)(2,1)S(1)}, bf16[256,4,128]{2,0,1:T(8,128)(2,1)}, u32[]{:S(2)}, u32[]{:S(2)}) collective-permute-start(bf16[256,4,128]{2,0,1:T(8,128)(2,1)S(1)} %bitcast.95), channel_id=1, source_target_pairs={{0,4},{4,8},{8,12},{12,16},{16,20},{20,24},{24,28},{1,5},{5,9},{9,... | collective-permute-start | bytes 786440 | tf_op jit(solution)/shard_map/while/body/eval_jaxpr/ppermute | solution.py:12
  118.5 11.6 %copy-start.1 = (bf16[256,8,128]{2,0,1:T(8,128)(2,1)}, bf16[256,8,128]{2,0,1:T(8,128)(2,1)S(1)}, u32[]{:S(2)}) copy-start(bf16[256,8,128]{2,0,1:T(8,128)(2,1)S(1)} %convert_element_type.26) | copy-start | bytes 1572868 | tf_op jit(solution)/shard_map/while
  119.1 11.0 %collective-permute-start = (bf16[256,4,128]{2,0,1:T(8,128)(2,1)S(1)}, bf16[256,4,128]{2,0,1:T(8,128)(2,1)S(1)}, u32[]{:S(2)}, u32[]{:S(2)}) collective-permute-start(bf16[256,4,128]{2,0,1:T(8,128)(2,1)S(1)} %bitcast.94), channel_id=1, source_target_pairs={{4,0},{8,4},{12,8},{16,12},{20,16},{24,20},{28,24},{5,1},{9,5},{13... | collective-permute-start | bytes 786440 | tf_op jit(solution)/shard_map/while/body/eval_jaxpr/ppermute | solution.py:12
  121.1 14.8 %collective-permute-start.1 = (bf16[256,4,128]{2,0,1:T(8,128)(2,1)S(1)}, bf16[256,4,128]{2,0,1:T(8,128)(2,1)}, u32[]{:S(2)}, u32[]{:S(2)}) collective-permute-start(bf16[256,4,128]{2,0,1:T(8,128)(2,1)S(1)} %bitcast.95), channel_id=1, source_target_pairs={{0,4},{4,8},{8,12},{12,16},{16,20},{20,24},{24,28},{1,5},{5,9},{9,... | collective-permute-start | bytes 786440 | tf_op jit(solution)/shard_map/while/body/eval_jaxpr/ppermute | solution.py:12
  152.1 11.6 %copy-start.1 = (bf16[256,8,128]{2,0,1:T(8,128)(2,1)}, bf16[256,8,128]{2,0,1:T(8,128)(2,1)S(1)}, u32[]{:S(2)}) copy-start(bf16[256,8,128]{2,0,1:T(8,128)(2,1)S(1)} %convert_element_type.26) | copy-start | bytes 1572868 | tf_op jit(solution)/shard_map/while
  152.7 11.0 %collective-permute-start = (bf16[256,4,128]{2,0,1:T(8,128)(2,1)S(1)}, bf16[256,4,128]{2,0,1:T(8,128)(2,1)S(1)}, u32[]{:S(2)}, u32[]{:S(2)}) collective-permute-start(bf16[256,4,128]{2,0,1:T(8,128)(2,1)S(1)} %bitcast.94), channel_id=1, source_target_pairs={{4,0},{8,4},{12,8},{16,12},{20,16},{24,20},{28,24},{5,1},{9,5},{13... | collective-permute-start | bytes 786440 | tf_op jit(solution)/shard_map/while/body/eval_jaxpr/ppermute | solution.py:12
  154.6 14.8 %collective-permute-start.1 = (bf16[256,4,128]{2,0,1:T(8,128)(2,1)S(1)}, bf16[256,4,128]{2,0,1:T(8,128)(2,1)}, u32[]{:S(2)}, u32[]{:S(2)}) collective-permute-start(bf16[256,4,128]{2,0,1:T(8,128)(2,1)S(1)} %bitcast.95), channel_id=1, source_target_pairs={{0,4},{4,8},{8,12},{12,16},{16,20},{20,24},{24,28},{1,5},{5,9},{9,... | collective-permute-start | bytes 786440 | tf_op jit(solution)/shard_map/while/body/eval_jaxpr/ppermute | solution.py:12
  185.6 11.6 %copy-start.1 = (bf16[256,8,128]{2,0,1:T(8,128)(2,1)}, bf16[256,8,128]{2,0,1:T(8,128)(2,1)S(1)}, u32[]{:S(2)}) copy-start(bf16[256,8,128]{2,0,1:T(8,128)(2,1)S(1)} %convert_element_type.26) | copy-start | bytes 1572868 | tf_op jit(solution)/shard_map/while
  186.2 11.0 %collective-permute-start = (bf16[256,4,128]{2,0,1:T(8,128)(2,1)S(1)}, bf16[256,4,128]{2,0,1:T(8,128)(2,1)S(1)}, u32[]{:S(2)}, u32[]{:S(2)}) collective-permute-start(bf16[256,4,128]{2,0,1:T(8,128)(2,1)S(1)} %bitcast.94), channel_id=1, source_target_pairs={{4,0},{8,4},{12,8},{16,12},{20,16},{24,20},{28,24},{5,1},{9,5},{13... | collective-permute-start | bytes 786440 | tf_op jit(solution)/shard_map/while/body/eval_jaxpr/ppermute | solution.py:12
  188.2 14.8 %collective-permute-start.1 = (bf16[256,4,128]{2,0,1:T(8,128)(2,1)S(1)}, bf16[256,4,128]{2,0,1:T(8,128)(2,1)}, u32[]{:S(2)}, u32[]{:S(2)}) collective-permute-start(bf16[256,4,128]{2,0,1:T(8,128)(2,1)S(1)} %bitcast.95), channel_id=1, source_target_pairs={{0,4},{4,8},{8,12},{12,16},{16,20},{20,24},{24,28},{1,5},{5,9},{9,... | collective-permute-start | bytes 786440 | tf_op jit(solution)/shard_map/while/body/eval_jaxpr/ppermute | solution.py:12
  219.2 11.6 %copy-start.1 = (bf16[256,8,128]{2,0,1:T(8,128)(2,1)}, bf16[256,8,128]{2,0,1:T(8,128)(2,1)S(1)}, u32[]{:S(2)}) copy-start(bf16[256,8,128]{2,0,1:T(8,128)(2,1)S(1)} %convert_element_type.26) | copy-start | bytes 1572868 | tf_op jit(solution)/shard_map/while
  219.8 11.0 %collective-permute-start = (bf16[256,4,128]{2,0,1:T(8,128)(2,1)S(1)}, bf16[256,4,128]{2,0,1:T(8,128)(2,1)S(1)}, u32[]{:S(2)}, u32[]{:S(2)}) collective-permute-start(bf16[256,4,128]{2,0,1:T(8,128)(2,1)S(1)} %bitcast.94), channel_id=1, source_target_pairs={{4,0},{8,4},{12,8},{16,12},{20,16},{24,20},{28,24},{5,1},{9,5},{13... | collective-permute-start | bytes 786440 | tf_op jit(solution)/shard_map/while/body/eval_jaxpr/ppermute | solution.py:12
  221.7 14.8 %collective-permute-start.1 = (bf16[256,4,128]{2,0,1:T(8,128)(2,1)S(1)}, bf16[256,4,128]{2,0,1:T(8,128)(2,1)}, u32[]{:S(2)}, u32[]{:S(2)}) collective-permute-start(bf16[256,4,128]{2,0,1:T(8,128)(2,1)S(1)} %bitcast.95), channel_id=1, source_target_pairs={{0,4},{4,8},{8,12},{12,16},{16,20},{20,24},{24,28},{1,5},{5,9},{9,... | collective-permute-start | bytes 786440 | tf_op jit(solution)/shard_map/while/body/eval_jaxpr/ppermute | solution.py:12
  252.7 11.6 %copy-start.1 = (bf16[256,8,128]{2,0,1:T(8,128)(2,1)}, bf16[256,8,128]{2,0,1:T(8,128)(2,1)S(1)}, u32[]{:S(2)}) copy-start(bf16[256,8,128]{2,0,1:T(8,128)(2,1)S(1)} %convert_element_type.26) | copy-start | bytes 1572868 | tf_op jit(solution)/shard_map/while
  253.3 11.0 %collective-permute-start = (bf16[256,4,128]{2,0,1:T(8,128)(2,1)S(1)}, bf16[256,4,128]{2,0,1:T(8,128)(2,1)S(1)}, u32[]{:S(2)}, u32[]{:S(2)}) collective-permute-start(bf16[256,4,128]{2,0,1:T(8,128)(2,1)S(1)} %bitcast.94), channel_id=1, source_target_pairs={{4,0},{8,4},{12,8},{16,12},{20,16},{24,20},{28,24},{5,1},{9,5},{13... | collective-permute-start | bytes 786440 | tf_op jit(solution)/shard_map/while/body/eval_jaxpr/ppermute | solution.py:12
  255.3 14.8 %collective-permute-start.1 = (bf16[256,4,128]{2,0,1:T(8,128)(2,1)S(1)}, bf16[256,4,128]{2,0,1:T(8,128)(2,1)}, u32[]{:S(2)}, u32[]{:S(2)}) collective-permute-start(bf16[256,4,128]{2,0,1:T(8,128)(2,1)S(1)} %bitcast.95), channel_id=1, source_target_pairs={{0,4},{4,8},{8,12},{12,16},{16,20},{20,24},{24,28},{1,5},{5,9},{9,... | collective-permute-start | bytes 786440 | tf_op jit(solution)/shard_map/while/body/eval_jaxpr/ppermute | solution.py:12
  286.3 11.6 %copy-start.1 = (bf16[256,8,128]{2,0,1:T(8,128)(2,1)}, bf16[256,8,128]{2,0,1:T(8,128)(2,1)S(1)}, u32[]{:S(2)}) copy-start(bf16[256,8,128]{2,0,1:T(8,128)(2,1)S(1)} %convert_element_type.26) | copy-start | bytes 1572868 | tf_op jit(solution)/shard_map/while
  286.9 11.0 %collective-permute-start = (bf16[256,4,128]{2,0,1:T(8,128)(2,1)S(1)}, bf16[256,4,128]{2,0,1:T(8,128)(2,1)S(1)}, u32[]{:S(2)}, u32[]{:S(2)}) collective-permute-start(bf16[256,4,128]{2,0,1:T(8,128)(2,1)S(1)} %bitcast.94), channel_id=1, source_target_pairs={{4,0},{8,4},{12,8},{16,12},{20,16},{24,20},{28,24},{5,1},{9,5},{13... | collective-permute-start | bytes 786440 | tf_op jit(solution)/shard_map/while/body/eval_jaxpr/ppermute | solution.py:12
  288.8 14.8 %collective-permute-start.1 = (bf16[256,4,128]{2,0,1:T(8,128)(2,1)S(1)}, bf16[256,4,128]{2,0,1:T(8,128)(2,1)}, u32[]{:S(2)}, u32[]{:S(2)}) collective-permute-start(bf16[256,4,128]{2,0,1:T(8,128)(2,1)S(1)} %bitcast.95), channel_id=1, source_target_pairs={{0,4},{4,8},{8,12},{12,16},{16,20},{20,24},{24,28},{1,5},{5,9},{9,... | collective-permute-start | bytes 786440 | tf_op jit(solution)/shard_map/while/body/eval_jaxpr/ppermute | solution.py:12
  319.8 11.6 %copy-start.1 = (bf16[256,8,128]{2,0,1:T(8,128)(2,1)}, bf16[256,8,128]{2,0,1:T(8,128)(2,1)S(1)}, u32[]{:S(2)}) copy-start(bf16[256,8,128]{2,0,1:T(8,128)(2,1)S(1)} %convert_element_type.26) | copy-start | bytes 1572868 | tf_op jit(solution)/shard_map/while
  320.5 11.0 %collective-permute-start = (bf16[256,4,128]{2,0,1:T(8,128)(2,1)S(1)}, bf16[256,4,128]{2,0,1:T(8,128)(2,1)S(1)}, u32[]{:S(2)}, u32[]{:S(2)}) collective-permute-start(bf16[256,4,128]{2,0,1:T(8,128)(2,1)S(1)} %bitcast.94), channel_id=1, source_target_pairs={{4,0},{8,4},{12,8},{16,12},{20,16},{24,20},{28,24},{5,1},{9,5},{13... | collective-permute-start | bytes 786440 | tf_op jit(solution)/shard_map/while/body/eval_jaxpr/ppermute | solution.py:12
  322.4 14.8 %collective-permute-start.1 = (bf16[256,4,128]{2,0,1:T(8,128)(2,1)S(1)}, bf16[256,4,128]{2,0,1:T(8,128)(2,1)}, u32[]{:S(2)}, u32[]{:S(2)}) collective-permute-start(bf16[256,4,128]{2,0,1:T(8,128)(2,1)S(1)} %bitcast.95), channel_id=1, source_target_pairs={{0,4},{4,8},{8,12},{12,16},{16,20},{20,24},{24,28},{1,5},{5,9},{9,... | collective-permute-start | bytes 786440 | tf_op jit(solution)/shard_map/while/body/eval_jaxpr/ppermute | solution.py:12
  353.4 11.6 %copy-start.1 = (bf16[256,8,128]{2,0,1:T(8,128)(2,1)}, bf16[256,8,128]{2,0,1:T(8,128)(2,1)S(1)}, u32[]{:S(2)}) copy-start(bf16[256,8,128]{2,0,1:T(8,128)(2,1)S(1)} %convert_element_type.26) | copy-start | bytes 1572868 | tf_op jit(solution)/shard_map/while
  354.0 11.0 %collective-permute-start = (bf16[256,4,128]{2,0,1:T(8,128)(2,1)S(1)}, bf16[256,4,128]{2,0,1:T(8,128)(2,1)S(1)}, u32[]{:S(2)}, u32[]{:S(2)}) collective-permute-start(bf16[256,4,128]{2,0,1:T(8,128)(2,1)S(1)} %bitcast.94), channel_id=1, source_target_pairs={{4,0},{8,4},{12,8},{16,12},{20,16},{24,20},{28,24},{5,1},{9,5},{13... | collective-permute-start | bytes 786440 | tf_op jit(solution)/shard_map/while/body/eval_jaxpr/ppermute | solution.py:12
  355.9 14.8 %collective-permute-start.1 = (bf16[256,4,128]{2,0,1:T(8,128)(2,1)S(1)}, bf16[256,4,128]{2,0,1:T(8,128)(2,1)}, u32[]{:S(2)}, u32[]{:S(2)}) collective-permute-start(bf16[256,4,128]{2,0,1:T(8,128)(2,1)S(1)} %bitcast.95), channel_id=1, source_target_pairs={{0,4},{4,8},{8,12},{12,16},{16,20},{20,24},{24,28},{1,5},{5,9},{9,... | collective-permute-start | bytes 786440 | tf_op jit(solution)/shard_map/while/body/eval_jaxpr/ppermute | solution.py:12
  (1 other events, 6.9 us)
Sparse Core Ops, SparseCore 0:
  8.9 37.1 all-gather.1
where the time goes:
time: 396 us; the launch traced here: 395 us
  waiting for transfers between devices  122 us (31%)
  local copies, waits for them, and re-layouts  89 us (22%)
  matrix products  80.4 us (20%)
  starting transfers between devices  68.7 us (17%)
  other arithmetic  19.9 us (5%)
  between operations  14.1 us (4%)
    ppermute x20, waiting for transfers between devices, passed_along(): return lax.ppermute(x, axis, pairs)  83.5 us
    dot_general x10, matrix products, apply_blocks(): jnp.einsum('cbkj,bkij->cbi', picked, blocks, preferred_element_type=jnp.f...  71.6 us
    ppermute x20, starting transfers between devices, passed_along(): return lax.ppermute(x, axis, pairs)  68.7 us
    gather x10, local copies, waits for them, and re-layouts, apply_blocks(): picked = source[:, cols, :]  65.7 us
    all_gather x1, waiting for transfers between devices, body(): lax.all_gather(vectors, 'col', axis=0, tiled=True)  37.4 us
    concatenate x10, other arithmetic, apply_blocks(): source = jnp.concatenate([from_prev, lowered, from_next], axis=1)  11.2 us
    while x36, local copies, waits for them, and re-layouts  9.43 us
    dot_general x1, matrix products, body(): lax.dot_general(rotation, lax.all_gather(vectors, 'col', axis=0, tiled=Tr...  8.72 us
  transfers between devices with their start and end apart: 21, of which 20 were waited for; matrix products, arithmetic and copies ran while one was open for 3% of the time, Pallas kernels for 0%

commit v1 on v0

--- a/solution.py
+++ b/solution.py
@@ -4,6 +4,19 @@
 from jax.sharding import PartitionSpec as P
 
 STEPS = 10
+
+
+def collect(value, axis, dim):
+    size, mine, span = (lax.axis_size(axis), lax.axis_index(axis), value.shape[dim])
+    right = [(i, (i + 1) % size) for i in range(size)]
+    result = jnp.zeros((*value.shape[:dim], size * span, *value.shape[dim + 1 :]), value.dtype)
+    held = value
+    for turn in range(size):
+        owner = (mine - turn) % size
+        result = lax.dynamic_update_slice_in_dim(result, held, owner * span, axis=dim)
+        if turn < size - 1:
+            held = lax.ppermute(held, axis, right)
+    return result
 
 
 def passed_along(x, axis, by):
@@ -29,7 +42,7 @@
     width = blocks.shape[2]
     panel = lax.dot_general(
         rotation,
-        lax.all_gather(vectors, "col", axis=0, tiled=True),
+        collect(vectors, "col", 0),
         (((0,), (1,)), ((), ())),
         precision=lax.Precision.HIGHEST,
         preferred_element_type=jnp.float32,

time: 396 us -> 383 us (0.967)
  between operations: 14.1 us -> 0.83 us
  matrix products: 80.4 us -> 75.1 us
    ppermute x0 -> x3, waiting for transfers between devices: none -> 40 us  [collect(): held = lax.ppermute(held, axis, right)]
    all_gather x1 -> x0, waiting for transfers between devices: 37.4 us -> none  [body(): lax.all_gather(vectors, 'col', axis=0, tiled=True)]
    dot_general x1, matrix products: 8.72 us -> 3.42 us  [body(): lax.dot_general(rotation, collect(vectors, 'col', 0), (((0,), (1,)), ((),...]
  transfers between devices with their start and end apart: 21 -> 23, of which waited for: 20 -> 22; matrix products, arithmetic and copies ran while one was open for 3% -> 4% of each run, Pallas kernels for 0% -> 0%
where the time goes in v1:
time: 383 us; the launch traced here: 380 us
  waiting for transfers between devices  121 us (32%)
  local copies, waits for them, and re-layouts  92.6 us (24%)
  matrix products  75.1 us (20%)
  starting transfers between devices  70.1 us (18%)
  other arithmetic  19.9 us (5%)
    ppermute x20, waiting for transfers between devices, passed_along(): return lax.ppermute(x, axis, pairs)  80.5 us
    dot_general x10, matrix products, apply_blocks(): jnp.einsum('cbkj,bkij->cbi', picked, blocks, preferred_element_type=jnp.f...  71.7 us
    ppermute x20, starting transfers between devices, passed_along(): return lax.ppermute(x, axis, pairs)  69.6 us
    gather x10, local copies, waits for them, and re-layouts, apply_blocks(): picked = source[:, cols, :]  65.7 us
    ppermute x3, waiting for transfers between devices, collect(): held = lax.ppermute(held, axis, right)  40 us
    concatenate x10, other arithmetic, apply_blocks(): source = jnp.concatenate([from_prev, lowered, from_next], axis=1)  11.2 us
    while x36, local copies, waits for them, and re-layouts  9.43 us
  transfers between devices with their start and end apart: 23, of which 22 were waited for; matrix products, arithmetic and copies ran while one was open for 4% of the time, Pallas kernels for 0%

profile of v1, /device:TPU:0, one launch (start us, length us, event | category | flops | bytes accessed | tf_op | source)
XLA Modules:
  0.0 380.0 jit_solution(8962396059297481968)
XLA Ops:
  0.5 14.7 %collective-permute-done.2 = f32[256,1024]{1,0:T(8,128)S(1)} collective-permute-done((f32[256,1024]{1,0:T(8,128)}, f32[256,1024]{1,0:T(8,128)S(1)}, u32[]{:S(2)}, u32[]{:S(2)}) %collective-permute-start.2) | collective-permute-done | bytes 1048608 | tf_op jit(solution)/shard_map/ppermute | solution.py:18
  15.2 14.3 %collective-permute-done.3 = f32[256,1024]{1,0:T(8,128)} collective-permute-done((f32[256,1024]{1,0:T(8,128)S(1)}, f32[256,1024]{1,0:T(8,128)}, u32[]{:S(2)}, u32[]{:S(2)}) %collective-permute-start.3) | collective-permute-done | bytes 1048608 | tf_op jit(solution)/shard_map/ppermute | solution.py:18
  33.0 11.1 %collective-permute-done.4 = f32[256,1024]{1,0:T(8,128)} collective-permute-done((f32[256,1024]{1,0:T(8,128)}, f32[256,1024]{1,0:T(8,128)}, u32[]{:S(2)}, u32[]{:S(2)}) %collective-permute-start.4) | collective-permute-done | bytes 1048608 | tf_op jit(solution)/shard_map/ppermute | solution.py:18
  57.3 8.3 %collective-permute-done.5 = bf16[256,4,128]{2,0,1:T(8,128)(2,1)S(1)} collective-permute-done((bf16[256,4,128]{2,0,1:T(8,128)(2,1)S(1)}, bf16[256,4,128]{2,0,1:T(8,128)(2,1)S(1)}, u32[]{:S(2)}, u32[]{:S(2)}) %collective-permute-start.5) | collective-permute-done | bytes 262176 | tf_op jit(solution)/shard_map/ppermute | solution.py:25
  65.7 6.6 %gather_fusion.5 = bf16[128,256,128]{2,1,0:T(8,128)(2,1)} fusion(bf16[256,16,128]{2,0,1:T(8,128)(2,1)S(1)} %pad_maximum_fusion.1, s32[1024]{0:T(1024)S(1)} %pad_clamp_fusion.3), kind=kCustom, calls=%fused_computation.5 | custom fusion | bytes 16777728 | tf_op jit(solution)/shard_map/gather | solution.py:35
  72.3 6.9 %fusion.9 = f32[256,8,128]{2,0,1:T(8,128)S(1)} fusion(bf16[256,8,16,128]{3,0,2,1:T(8,128)(2,1)} %bitcast.91, bf16[8,16,128,128]{3,2,1,0:T(8,128)(2,1)} %param.10, f32[8]{0:T(128)S(1)} %compare_convert_fusion.1), kind=kOutput, calls=%fused_computation.24 | convolution fusion | flops 1074003968 | bytes 13631520 | tf_op jit(solution)/shard_map/cbkj,bkij->cbi/dot_general | solution.py:36
  79.2 299.7 %while.13 = (s32[]{:T(128)}, f32[256,8,128]{2,0,1:T(8,128)}, f32[256,8,128]{2,0,1:T(8,128)S(1)}, s32[1,2,4]{2,1,0:T(2,128)S(1)}, s32[8,16]{1,0:T(8,128)S(1)}, /*...) while((s32[]{:T(128)}, f32[256,8,128]{2,0,1:T(8,128)}, f32[256,8,128]{2,0,1:T(8,128)S(1)}, ...), condition=%wide.region_1.2_spmd.clone, body=%wide.region_0.1_spmd.clone.sunk | while | flops 1075842432 | bytes 44580228 | solution.py:59
  88.7 6.7 %collective-permute-done.1 = bf16[256,4,128]{2,0,1:T(8,128)(2,1)} collective-permute-done((bf16[256,4,128]{2,0,1:T(8,128)(2,1)S(1)}, bf16[256,4,128]{2,0,1:T(8,128)(2,1)}, u32[]{:S(2)}, u32[]{:S(2)}) %collective-permute-start.1) | collective-permute-done | bytes 262176 | tf_op jit(solution)/shard_map/while/body/eval_jaxpr/ppermute | solution.py:25
  96.6 6.6 %gather_fusion.2 = bf16[128,256,128]{2,1,0:T(8,128)(2,1)} fusion(bf16[256,16,128]{2,0,1:T(8,128)(2,1)S(1)} %pad_maximum_fusion.3, s32[1024]{0:T(1024)S(1)} %pad_clamp_fusion.9), kind=kCustom, calls=%fused_computation.2.clone.clone.1 | custom fusion | bytes 16777728 | tf_op jit(solution)/shard_map/while/body/eval_jaxpr/gather | solution.py:35
  103.2 7.2 %fusion.28 = f32[256,8,128]{2,0,1:T(8,128)S(1)} fusion(f32[256,8,128]{2,0,1:T(8,128)} %get-tuple-element.144, bf16[256,8,16,128]{3,0,2,1:T(8,128)(2,1)} %bitcast.90, bf16[8,16,128,128]{3,2,1,0:T(8,128)(2,1)} %get-tuple-element.156, f32[8]{0:T(128)S(1)} %compare_convert_fusion.3), kind=kOutput, calls=%fused_computation.11.clone.1 | convolution fusion | flops 1074528256 | bytes 14680096 | tf_op jit(solution)/shard_map/while/body/eval_jaxpr/cbkj,bkij->cbi/dot_general | solution.py:36
  114.1 5.8 %collective-permute-start.1 = (bf16[256,4,128]{2,0,1:T(8,128)(2,1)S(1)}, bf16[256,4,128]{2,0,1:T(8,128)(2,1)}, u32[]{:S(2)}, u32[]{:S(2)}) collective-permute-start(bf16[256,4,128]{2,0,1:T(8,128)(2,1)S(1)} %bitcast.93), channel_id=1, source_target_pairs={{0,4},{4,8},{8,12},{12,16},{16,20},{20,24},{24,28},{1,5},{5,9},{9,... | collective-permute-start | bytes 786440 | tf_op jit(solution)/shard_map/while/body/eval_jaxpr/ppermute | solution.py:25
  122.1 5.9 %collective-permute-done.1 = bf16[256,4,128]{2,0,1:T(8,128)(2,1)} collective-permute-done((bf16[256,4,128]{2,0,1:T(8,128)(2,1)S(1)}, bf16[256,4,128]{2,0,1:T(8,128)(2,1)}, u32[]{:S(2)}, u32[]{:S(2)}) %collective-permute-start.1) | collective-permute-done | bytes 262176 | tf_op jit(solution)/shard_map/while/body/eval_jaxpr/ppermute | solution.py:25
  129.3 6.6 %gather_fusion.2 = bf16[128,256,128]{2,1,0:T(8,128)(2,1)} fusion(bf16[256,16,128]{2,0,1:T(8,128)(2,1)S(1)} %pad_maximum_fusion.3, s32[1024]{0:T(1024)S(1)} %pad_clamp_fusion.9), kind=kCustom, calls=%fused_computation.2.clone.clone.1 | custom fusion | bytes 16777728 | tf_op jit(solution)/shard_map/while/body/eval_jaxpr/gather | solution.py:35
  135.9 7.2 %fusion.28 = f32[256,8,128]{2,0,1:T(8,128)S(1)} fusion(f32[256,8,128]{2,0,1:T(8,128)} %get-tuple-element.144, bf16[256,8,16,128]{3,0,2,1:T(8,128)(2,1)} %bitcast.90, bf16[8,16,128,128]{3,2,1,0:T(8,128)(2,1)} %get-tuple-element.156, f32[8]{0:T(128)S(1)} %compare_convert_fusion.3), kind=kOutput, calls=%fused_computation.11.clone.1 | convolution fusion | flops 1074528256 | bytes 14680096 | tf_op jit(solution)/shard_map/while/body/eval_jaxpr/cbkj,bkij->cbi/dot_general | solution.py:36
  162.8 6.6 %gather_fusion.2 = bf16[128,256,128]{2,1,0:T(8,128)(2,1)} fusion(bf16[256,16,128]{2,0,1:T(8,128)(2,1)S(1)} %pad_maximum_fusion.3, s32[1024]{0:T(1024)S(1)} %pad_clamp_fusion.9), kind=kCustom, calls=%fused_computation.2.clone.clone.1 | custom fusion | bytes 16777728 | tf_op jit(solution)/shard_map/while/body/eval_jaxpr/gather | solution.py:35
  169.4 7.2 %fusion.28 = f32[256,8,128]{2,0,1:T(8,128)S(1)} fusion(f32[256,8,128]{2,0,1:T(8,128)} %get-tuple-element.144, bf16[256,8,16,128]{3,0,2,1:T(8,128)(2,1)} %bitcast.90, bf16[8,16,128,128]{3,2,1,0:T(8,128)(2,1)} %get-tuple-element.156, f32[8]{0:T(128)S(1)} %compare_convert_fusion.3), kind=kOutput, calls=%fused_computation.11.clone.1 | convolution fusion | flops 1074528256 | bytes 14680096 | tf_op jit(solution)/shard_map/while/body/eval_jaxpr/cbkj,bkij->cbi/dot_general | solution.py:36
  180.3 5.8 %collective-permute-start.1 = (bf16[256,4,128]{2,0,1:T(8,128)(2,1)S(1)}, bf16[256,4,128]{2,0,1:T(8,128)(2,1)}, u32[]{:S(2)}, u32[]{:S(2)}) collective-permute-start(bf16[256,4,128]{2,0,1:T(8,128)(2,1)S(1)} %bitcast.93), channel_id=1, source_target_pairs={{0,4},{4,8},{8,12},{12,16},{16,20},{20,24},{24,28},{1,5},{5,9},{9,... | collective-permute-start | bytes 786440 | tf_op jit(solution)/shard_map/while/body/eval_jaxpr/ppermute | solution.py:25
  196.4 6.6 %gather_fusion.2 = bf16[128,256,128]{2,1,0:T(8,128)(2,1)} fusion(bf16[256,16,128]{2,0,1:T(8,128)(2,1)S(1)} %pad_maximum_fusion.3, s32[1024]{0:T(1024)S(1)} %pad_clamp_fusion.9), kind=kCustom, calls=%fused_computation.2.clone.clone.1 | custom fusion | bytes 16777728 | tf_op jit(solution)/shard_map/while/body/eval_jaxpr/gather | solution.py:35
  203.0 7.2 %fusion.28 = f32[256,8,128]{2,0,1:T(8,128)S(1)} fusion(f32[256,8,128]{2,0,1:T(8,128)} %get-tuple-element.144, bf16[256,8,16,128]{3,0,2,1:T(8,128)(2,1)} %bitcast.90, bf16[8,16,128,128]{3,2,1,0:T(8,128)(2,1)} %get-tuple-element.156, f32[8]{0:T(128)S(1)} %compare_convert_fusion.3), kind=kOutput, calls=%fused_computation.11.clone.1 | convolution fusion | flops 1074528256 | bytes 14680096 | tf_op jit(solution)/shard_map/while/body/eval_jaxpr/cbkj,bkij->cbi/dot_general | solution.py:36
  213.9 5.8 %collective-permute-start.1 = (bf16[256,4,128]{2,0,1:T(8,128)(2,1)S(1)}, bf16[256,4,128]{2,0,1:T(8,128)(2,1)}, u32[]{:S(2)}, u32[]{:S(2)}) collective-permute-start(bf16[256,4,128]{2,0,1:T(8,128)(2,1)S(1)} %bitcast.93), channel_id=1, source_target_pairs={{0,4},{4,8},{8,12},{12,16},{16,20},{20,24},{24,28},{1,5},{5,9},{9,... | collective-permute-start | bytes 786440 | tf_op jit(solution)/shard_map/while/body/eval_jaxpr/ppermute | solution.py:25
  229.9 6.6 %gather_fusion.2 = bf16[128,256,128]{2,1,0:T(8,128)(2,1)} fusion(bf16[256,16,128]{2,0,1:T(8,128)(2,1)S(1)} %pad_maximum_fusion.3, s32[1024]{0:T(1024)S(1)} %pad_clamp_fusion.9), kind=kCustom, calls=%fused_computation.2.clone.clone.1 | custom fusion | bytes 16777728 | tf_op jit(solution)/shard_map/while/body/eval_jaxpr/gather | solution.py:35
  236.5 7.2 %fusion.28 = f32[256,8,128]{2,0,1:T(8,128)S(1)} fusion(f32[256,8,128]{2,0,1:T(8,128)} %get-tuple-element.144, bf16[256,8,16,128]{3,0,2,1:T(8,128)(2,1)} %bitcast.90, bf16[8,16,128,128]{3,2,1,0:T(8,128)(2,1)} %get-tuple-element.156, f32[8]{0:T(128)S(1)} %compare_convert_fusion.3), kind=kOutput, calls=%fused_computation.11.clone.1 | convolution fusion | flops 1074528256 | bytes 14680096 | tf_op jit(solution)/shard_map/while/body/eval_jaxpr/cbkj,bkij->cbi/dot_general | solution.py:36
  263.5 6.6 %gather_fusion.2 = bf16[128,256,128]{2,1,0:T(8,128)(2,1)} fusion(bf16[256,16,128]{2,0,1:T(8,128)(2,1)S(1)} %pad_maximum_fusion.3, s32[1024]{0:T(1024)S(1)} %pad_clamp_fusion.9), kind=kCustom, calls=%fused_computation.2.clone.clone.1 | custom fusion | bytes 16777728 | tf_op jit(solution)/shard_map/while/body/eval_jaxpr/gather | solution.py:35
  270.0 7.2 %fusion.28 = f32[256,8,128]{2,0,1:T(8,128)S(1)} fusion(f32[256,8,128]{2,0,1:T(8,128)} %get-tuple-element.144, bf16[256,8,16,128]{3,0,2,1:T(8,128)(2,1)} %bitcast.90, bf16[8,16,128,128]{3,2,1,0:T(8,128)(2,1)} %get-tuple-element.156, f32[8]{0:T(128)S(1)} %compare_convert_fusion.3), kind=kOutput, calls=%fused_computation.11.clone.1 | convolution fusion | flops 1074528256 | bytes 14680096 | tf_op jit(solution)/shard_map/while/body/eval_jaxpr/cbkj,bkij->cbi/dot_general | solution.py:36
  281.0 5.8 %collective-permute-start.1 = (bf16[256,4,128]{2,0,1:T(8,128)(2,1)S(1)}, bf16[256,4,128]{2,0,1:T(8,128)(2,1)}, u32[]{:S(2)}, u32[]{:S(2)}) collective-permute-start(bf16[256,4,128]{2,0,1:T(8,128)(2,1)S(1)} %bitcast.93), channel_id=1, source_target_pairs={{0,4},{4,8},{8,12},{12,16},{16,20},{20,24},{24,28},{1,5},{5,9},{9,... | collective-permute-start | bytes 786440 | tf_op jit(solution)/shard_map/while/body/eval_jaxpr/ppermute | solution.py:25
  297.0 6.6 %gather_fusion.2 = bf16[128,256,128]{2,1,0:T(8,128)(2,1)} fusion(bf16[256,16,128]{2,0,1:T(8,128)(2,1)S(1)} %pad_maximum_fusion.3, s32[1024]{0:T(1024)S(1)} %pad_clamp_fusion.9), kind=kCustom, calls=%fused_computation.2.clone.clone.1 | custom fusion | bytes 16777728 | tf_op jit(solution)/shard_map/while/body/eval_jaxpr/gather | solution.py:35
  303.6 7.2 %fusion.28 = f32[256,8,128]{2,0,1:T(8,128)S(1)} fusion(f32[256,8,128]{2,0,1:T(8,128)} %get-tuple-element.144, bf16[256,8,16,128]{3,0,2,1:T(8,128)(2,1)} %bitcast.90, bf16[8,16,128,128]{3,2,1,0:T(8,128)(2,1)} %get-tuple-element.156, f32[8]{0:T(128)S(1)} %compare_convert_fusion.3), kind=kOutput, calls=%fused_computation.11.clone.1 | convolution fusion | flops 1074528256 | bytes 14680096 | tf_op jit(solution)/shard_map/while/body/eval_jaxpr/cbkj,bkij->cbi/dot_general | solution.py:36
  330.6 6.6 %gather_fusion.2 = bf16[128,256,128]{2,1,0:T(8,128)(2,1)} fusion(bf16[256,16,128]{2,0,1:T(8,128)(2,1)S(1)} %pad_maximum_fusion.3, s32[1024]{0:T(1024)S(1)} %pad_clamp_fusion.9), kind=kCustom, calls=%fused_computation.2.clone.clone.1 | custom fusion | bytes 16777728 | tf_op jit(solution)/shard_map/while/body/eval_jaxpr/gather | solution.py:35
  337.1 7.2 %fusion.28 = f32[256,8,128]{2,0,1:T(8,128)S(1)} fusion(f32[256,8,128]{2,0,1:T(8,128)} %get-tuple-element.144, bf16[256,8,16,128]{3,0,2,1:T(8,128)(2,1)} %bitcast.90, bf16[8,16,128,128]{3,2,1,0:T(8,128)(2,1)} %get-tuple-element.156, f32[8]{0:T(128)S(1)} %compare_convert_fusion.3), kind=kOutput, calls=%fused_computation.11.clone.1 | convolution fusion | flops 1074528256 | bytes 14680096 | tf_op jit(solution)/shard_map/while/body/eval_jaxpr/cbkj,bkij->cbi/dot_general | solution.py:36
  348.0 5.8 %collective-permute-start.1 = (bf16[256,4,128]{2,0,1:T(8,128)(2,1)S(1)}, bf16[256,4,128]{2,0,1:T(8,128)(2,1)}, u32[]{:S(2)}, u32[]{:S(2)}) collective-permute-start(bf16[256,4,128]{2,0,1:T(8,128)(2,1)S(1)} %bitcast.93), channel_id=1, source_target_pairs={{0,4},{4,8},{8,12},{12,16},{16,20},{20,24},{24,28},{1,5},{5,9},{9,... | collective-permute-start | bytes 786440 | tf_op jit(solution)/shard_map/while/body/eval_jaxpr/ppermute | solution.py:25
  364.1 6.6 %gather_fusion.2 = bf16[128,256,128]{2,1,0:T(8,128)(2,1)} fusion(bf16[256,16,128]{2,0,1:T(8,128)(2,1)S(1)} %pad_maximum_fusion.3, s32[1024]{0:T(1024)S(1)} %pad_clamp_fusion.9), kind=kCustom, calls=%fused_computation.2.clone.clone.1 | custom fusion | bytes 16777728 | tf_op jit(solution)/shard_map/while/body/eval_jaxpr/gather | solution.py:35
  370.7 7.2 %fusion.28 = f32[256,8,128]{2,0,1:T(8,128)S(1)} fusion(f32[256,8,128]{2,0,1:T(8,128)} %get-tuple-element.144, bf16[256,8,16,128]{3,0,2,1:T(8,128)(2,1)} %bitcast.90, bf16[8,16,128,128]{3,2,1,0:T(8,128)(2,1)} %get-tuple-element.156, f32[8]{0:T(128)S(1)} %compare_convert_fusion.3), kind=kOutput, calls=%fused_computation.11.clone.1 | convolution fusion | flops 1074528256 | bytes 14680096 | tf_op jit(solution)/shard_map/while/body/eval_jaxpr/cbkj,bkij->cbi/dot_general | solution.py:36
  (187 shorter events, 150.8 us)
Async XLA Ops:
  0.0 45.3 %copy-start = (f32[1024,256]{1,0:T(8,128)S(1)}, f32[1024,256]{1,0:T(8,128)}, u32[]{:S(2)}) copy-start(f32[1024,256]{1,0:T(8,128)} %param.9) | copy-start | bytes 3145732
  0.0 31.5 %copy-start.2 = (f32[256,1024]{1,0:T(8,128)S(1)}, f32[256,1024]{1,0:T(8,128)}, u32[]{:S(2)}) copy-start(f32[256,1024]{1,0:T(8,128)} %param.8) | copy-start | bytes 3145732
  0.0 15.2 %collective-permute-start.2 = (f32[256,1024]{1,0:T(8,128)}, f32[256,1024]{1,0:T(8,128)S(1)}, u32[]{:S(2)}, u32[]{:S(2)}) collective-permute-start(f32[256,1024]{1,0:T(8,128)} %param.8), channel_id=1, source_target_pairs={{0,1},{1,2},{2,3},{3,0},{4,5},{5,6},{6,7},{7,4},{8,9},{9,10},{10,1... | collective-permute-start | bytes 3145736 | tf_op jit(solution)/shard_map/ppermute | solution.py:18
  15.2 14.3 %collective-permute-start.3 = (f32[256,1024]{1,0:T(8,128)S(1)}, f32[256,1024]{1,0:T(8,128)}, u32[]{:S(2)}, u32[]{:S(2)}) collective-permute-start(f32[256,1024]{1,0:T(8,128)S(1)} %collective-permute-done.2), channel_id=1, source_target_pairs={{0,1},{1,2},{2,3},{3,0},{4,5},{5,6},{6,7},{7,4},{8,9},{9,10},{10,1... | collective-permute-start | bytes 3145736 | tf_op jit(solution)/shard_map/ppermute | solution.py:18
  29.5 14.5 %collective-permute-start.4 = (f32[256,1024]{1,0:T(8,128)}, f32[256,1024]{1,0:T(8,128)}, u32[]{:S(2)}, u32[]{:S(2)}) collective-permute-start(f32[256,1024]{1,0:T(8,128)} %collective-permute-done.3), channel_id=1, source_target_pairs={{0,1},{1,2},{2,3},{3,0},{4,5},{5,6},{6,7},{7,4},{8,9},{9,10},{10,1... | collective-permute-start | bytes 3145736 | tf_op jit(solution)/shard_map/ppermute | solution.py:18
  50.9 14.6 %collective-permute-start.5 = (bf16[256,4,128]{2,0,1:T(8,128)(2,1)S(1)}, bf16[256,4,128]{2,0,1:T(8,128)(2,1)S(1)}, u32[]{:S(2)}, u32[]{:S(2)}) collective-permute-start(bf16[256,4,128]{2,0,1:T(8,128)(2,1)S(1)} %bitcast.95), channel_id=1, source_target_pairs={{0,4},{4,8},{8,12},{12,16},{16,20},{20,24},{24,28},{1,5},{5,9},{9,... | collective-permute-start | bytes 786440 | tf_op jit(solution)/shard_map/ppermute | solution.py:25
  55.7 9.9 %collective-permute-start.6 = (bf16[256,4,128]{2,0,1:T(8,128)(2,1)S(1)}, bf16[256,4,128]{2,0,1:T(8,128)(2,1)S(1)}, u32[]{:S(2)}, u32[]{:S(2)}) collective-permute-start(bf16[256,4,128]{2,0,1:T(8,128)(2,1)S(1)} %bitcast.96), channel_id=1, source_target_pairs={{4,0},{8,4},{12,8},{16,12},{20,16},{24,20},{28,24},{5,1},{9,5},{13... | collective-permute-start | bytes 786440 | tf_op jit(solution)/shard_map/ppermute | solution.py:25
  79.9 8.7 %collective-permute-start = (bf16[256,4,128]{2,0,1:T(8,128)(2,1)S(1)}, bf16[256,4,128]{2,0,1:T(8,128)(2,1)S(1)}, u32[]{:S(2)}, u32[]{:S(2)}) collective-permute-start(bf16[256,4,128]{2,0,1:T(8,128)(2,1)S(1)} %bitcast.92), channel_id=1, source_target_pairs={{4,0},{8,4},{12,8},{16,12},{20,16},{24,20},{28,24},{5,1},{9,5},{13... | collective-permute-start | bytes 786440 | tf_op jit(solution)/shard_map/while/body/eval_jaxpr/ppermute | solution.py:25
  81.9 13.5 %collective-permute-start.1 = (bf16[256,4,128]{2,0,1:T(8,128)(2,1)S(1)}, bf16[256,4,128]{2,0,1:T(8,128)(2,1)}, u32[]{:S(2)}, u32[]{:S(2)}) collective-permute-start(bf16[256,4,128]{2,0,1:T(8,128)(2,1)S(1)} %bitcast.93), channel_id=1, source_target_pairs={{0,4},{4,8},{8,12},{12,16},{16,20},{20,24},{24,28},{1,5},{5,9},{9,... | collective-permute-start | bytes 786440 | tf_op jit(solution)/shard_map/while/body/eval_jaxpr/ppermute | solution.py:25
  112.2 10.0 %collective-permute-start = (bf16[256,4,128]{2,0,1:T(8,128)(2,1)S(1)}, bf16[256,4,128]{2,0,1:T(8,128)(2,1)S(1)}, u32[]{:S(2)}, u32[]{:S(2)}) collective-permute-start(bf16[256,4,128]{2,0,1:T(8,128)(2,1)S(1)} %bitcast.92), channel_id=1, source_target_pairs={{4,0},{8,4},{12,8},{16,12},{20,16},{24,20},{28,24},{5,1},{9,5},{13... | collective-permute-start | bytes 786440 | tf_op jit(solution)/shard_map/while/body/eval_jaxpr/ppermute | solution.py:25
  114.1 14.0 %collective-permute-start.1 = (bf16[256,4,128]{2,0,1:T(8,128)(2,1)S(1)}, bf16[256,4,128]{2,0,1:T(8,128)(2,1)}, u32[]{:S(2)}, u32[]{:S(2)}) collective-permute-start(bf16[256,4,128]{2,0,1:T(8,128)(2,1)S(1)} %bitcast.93), channel_id=1, source_target_pairs={{0,4},{4,8},{8,12},{12,16},{16,20},{20,24},{24,28},{1,5},{5,9},{9,... | collective-permute-start | bytes 786440 | tf_op jit(solution)/shard_map/while/body/eval_jaxpr/ppermute | solution.py:25
  144.2 11.6 %copy-start.1 = (bf16[256,8,128]{2,0,1:T(8,128)(2,1)}, bf16[256,8,128]{2,0,1:T(8,128)(2,1)S(1)}, u32[]{:S(2)}) copy-start(bf16[256,8,128]{2,0,1:T(8,128)(2,1)S(1)} %convert_element_type.26) | copy-start | bytes 1572868 | tf_op jit(solution)/shard_map/while
  144.9 11.0 %collective-permute-start = (bf16[256,4,128]{2,0,1:T(8,128)(2,1)S(1)}, bf16[256,4,128]{2,0,1:T(8,128)(2,1)S(1)}, u32[]{:S(2)}, u32[]{:S(2)}) collective-permute-start(bf16[256,4,128]{2,0,1:T(8,128)(2,1)S(1)} %bitcast.92), channel_id=1, source_target_pairs={{4,0},{8,4},{12,8},{16,12},{20,16},{24,20},{28,24},{5,1},{9,5},{13... | collective-permute-start | bytes 786440 | tf_op jit(solution)/shard_map/while/body/eval_jaxpr/ppermute | solution.py:25
  146.8 14.8 %collective-permute-start.1 = (bf16[256,4,128]{2,0,1:T(8,128)(2,1)S(1)}, bf16[256,4,128]{2,0,1:T(8,128)(2,1)}, u32[]{:S(2)}, u32[]{:S(2)}) collective-permute-start(bf16[256,4,128]{2,0,1:T(8,128)(2,1)S(1)} %bitcast.93), channel_id=1, source_target_pairs={{0,4},{4,8},{8,12},{12,16},{16,20},{20,24},{24,28},{1,5},{5,9},{9,... | collective-permute-start | bytes 786440 | tf_op jit(solution)/shard_map/while/body/eval_jaxpr/ppermute | solution.py:25
  177.8 11.6 %copy-start.1 = (bf16[256,8,128]{2,0,1:T(8,128)(2,1)}, bf16[256,8,128]{2,0,1:T(8,128)(2,1)S(1)}, u32[]{:S(2)}) copy-start(bf16[256,8,128]{2,0,1:T(8,128)(2,1)S(1)} %convert_element_type.26) | copy-start | bytes 1572868 | tf_op jit(solution)/shard_map/while
  178.4 11.0 %collective-permute-start = (bf16[256,4,128]{2,0,1:T(8,128)(2,1)S(1)}, bf16[256,4,128]{2,0,1:T(8,128)(2,1)S(1)}, u32[]{:S(2)}, u32[]{:S(2)}) collective-permute-start(bf16[256,4,128]{2,0,1:T(8,128)(2,1)S(1)} %bitcast.92), channel_id=1, source_target_pairs={{4,0},{8,4},{12,8},{16,12},{20,16},{24,20},{28,24},{5,1},{9,5},{13... | collective-permute-start | bytes 786440 | tf_op jit(solution)/shard_map/while/body/eval_jaxpr/ppermute | solution.py:25
  180.3 14.8 %collective-permute-start.1 = (bf16[256,4,128]{2,0,1:T(8,128)(2,1)S(1)}, bf16[256,4,128]{2,0,1:T(8,128)(2,1)}, u32[]{:S(2)}, u32[]{:S(2)}) collective-permute-start(bf16[256,4,128]{2,0,1:T(8,128)(2,1)S(1)} %bitcast.93), channel_id=1, source_target_pairs={{0,4},{4,8},{8,12},{12,16},{16,20},{20,24},{24,28},{1,5},{5,9},{9,... | collective-permute-start | bytes 786440 | tf_op jit(solution)/shard_map/while/body/eval_jaxpr/ppermute | solution.py:25
  211.3 11.6 %copy-start.1 = (bf16[256,8,128]{2,0,1:T(8,128)(2,1)}, bf16[256,8,128]{2,0,1:T(8,128)(2,1)S(1)}, u32[]{:S(2)}) copy-start(bf16[256,8,128]{2,0,1:T(8,128)(2,1)S(1)} %convert_element_type.26) | copy-start | bytes 1572868 | tf_op jit(solution)/shard_map/while
  212.0 11.0 %collective-permute-start = (bf16[256,4,128]{2,0,1:T(8,128)(2,1)S(1)}, bf16[256,4,128]{2,0,1:T(8,128)(2,1)S(1)}, u32[]{:S(2)}, u32[]{:S(2)}) collective-permute-start(bf16[256,4,128]{2,0,1:T(8,128)(2,1)S(1)} %bitcast.92), channel_id=1, source_target_pairs={{4,0},{8,4},{12,8},{16,12},{20,16},{24,20},{28,24},{5,1},{9,5},{13... | collective-permute-start | bytes 786440 | tf_op jit(solution)/shard_map/while/body/eval_jaxpr/ppermute | solution.py:25
  213.9 14.8 %collective-permute-start.1 = (bf16[256,4,128]{2,0,1:T(8,128)(2,1)S(1)}, bf16[256,4,128]{2,0,1:T(8,128)(2,1)}, u32[]{:S(2)}, u32[]{:S(2)}) collective-permute-start(bf16[256,4,128]{2,0,1:T(8,128)(2,1)S(1)} %bitcast.93), channel_id=1, source_target_pairs={{0,4},{4,8},{8,12},{12,16},{16,20},{20,24},{24,28},{1,5},{5,9},{9,... | collective-permute-start | bytes 786440 | tf_op jit(solution)/shard_map/while/body/eval_jaxpr/ppermute | solution.py:25
  244.9 11.6 %copy-start.1 = (bf16[256,8,128]{2,0,1:T(8,128)(2,1)}, bf16[256,8,128]{2,0,1:T(8,128)(2,1)S(1)}, u32[]{:S(2)}) copy-start(bf16[256,8,128]{2,0,1:T(8,128)(2,1)S(1)} %convert_element_type.26) | copy-start | bytes 1572868 | tf_op jit(solution)/shard_map/while
  245.5 11.0 %collective-permute-start = (bf16[256,4,128]{2,0,1:T(8,128)(2,1)S(1)}, bf16[256,4,128]{2,0,1:T(8,128)(2,1)S(1)}, u32[]{:S(2)}, u32[]{:S(2)}) collective-permute-start(bf16[256,4,128]{2,0,1:T(8,128)(2,1)S(1)} %bitcast.92), channel_id=1, source_target_pairs={{4,0},{8,4},{12,8},{16,12},{20,16},{24,20},{28,24},{5,1},{9,5},{13... | collective-permute-start | bytes 786440 | tf_op jit(solution)/shard_map/while/body/eval_jaxpr/ppermute | solution.py:25
  247.4 14.8 %collective-permute-start.1 = (bf16[256,4,128]{2,0,1:T(8,128)(2,1)S(1)}, bf16[256,4,128]{2,0,1:T(8,128)(2,1)}, u32[]{:S(2)}, u32[]{:S(2)}) collective-permute-start(bf16[256,4,128]{2,0,1:T(8,128)(2,1)S(1)} %bitcast.93), channel_id=1, source_target_pairs={{0,4},{4,8},{8,12},{12,16},{16,20},{20,24},{24,28},{1,5},{5,9},{9,... | collective-permute-start | bytes 786440 | tf_op jit(solution)/shard_map/while/body/eval_jaxpr/ppermute | solution.py:25
  278.4 11.6 %copy-start.1 = (bf16[256,8,128]{2,0,1:T(8,128)(2,1)}, bf16[256,8,128]{2,0,1:T(8,128)(2,1)S(1)}, u32[]{:S(2)}) copy-start(bf16[256,8,128]{2,0,1:T(8,128)(2,1)S(1)} %convert_element_type.26) | copy-start | bytes 1572868 | tf_op jit(solution)/shard_map/while
  279.0 11.0 %collective-permute-start = (bf16[256,4,128]{2,0,1:T(8,128)(2,1)S(1)}, bf16[256,4,128]{2,0,1:T(8,128)(2,1)S(1)}, u32[]{:S(2)}, u32[]{:S(2)}) collective-permute-start(bf16[256,4,128]{2,0,1:T(8,128)(2,1)S(1)} %bitcast.92), channel_id=1, source_target_pairs={{4,0},{8,4},{12,8},{16,12},{20,16},{24,20},{28,24},{5,1},{9,5},{13... | collective-permute-start | bytes 786440 | tf_op jit(solution)/shard_map/while/body/eval_jaxpr/ppermute | solution.py:25
  281.0 14.8 %collective-permute-start.1 = (bf16[256,4,128]{2,0,1:T(8,128)(2,1)S(1)}, bf16[256,4,128]{2,0,1:T(8,128)(2,1)}, u32[]{:S(2)}, u32[]{:S(2)}) collective-permute-start(bf16[256,4,128]{2,0,1:T(8,128)(2,1)S(1)} %bitcast.93), channel_id=1, source_target_pairs={{0,4},{4,8},{8,12},{12,16},{16,20},{20,24},{24,28},{1,5},{5,9},{9,... | collective-permute-start | bytes 786440 | tf_op jit(solution)/shard_map/while/body/eval_jaxpr/ppermute | solution.py:25
  312.0 11.6 %copy-start.1 = (bf16[256,8,128]{2,0,1:T(8,128)(2,1)}, bf16[256,8,128]{2,0,1:T(8,128)(2,1)S(1)}, u32[]{:S(2)}) copy-start(bf16[256,8,128]{2,0,1:T(8,128)(2,1)S(1)} %convert_element_type.26) | copy-start | bytes 1572868 | tf_op jit(solution)/shard_map/while
  312.6 11.0 %collective-permute-start = (bf16[256,4,128]{2,0,1:T(8,128)(2,1)S(1)}, bf16[256,4,128]{2,0,1:T(8,128)(2,1)S(1)}, u32[]{:S(2)}, u32[]{:S(2)}) collective-permute-start(bf16[256,4,128]{2,0,1:T(8,128)(2,1)S(1)} %bitcast.92), channel_id=1, source_target_pairs={{4,0},{8,4},{12,8},{16,12},{20,16},{24,20},{28,24},{5,1},{9,5},{13... | collective-permute-start | bytes 786440 | tf_op jit(solution)/shard_map/while/body/eval_jaxpr/ppermute | solution.py:25
  314.5 14.8 %collective-permute-start.1 = (bf16[256,4,128]{2,0,1:T(8,128)(2,1)S(1)}, bf16[256,4,128]{2,0,1:T(8,128)(2,1)}, u32[]{:S(2)}, u32[]{:S(2)}) collective-permute-start(bf16[256,4,128]{2,0,1:T(8,128)(2,1)S(1)} %bitcast.93), channel_id=1, source_target_pairs={{0,4},{4,8},{8,12},{12,16},{16,20},{20,24},{24,28},{1,5},{5,9},{9,... | collective-permute-start | bytes 786440 | tf_op jit(solution)/shard_map/while/body/eval_jaxpr/ppermute | solution.py:25
  345.5 11.6 %copy-start.1 = (bf16[256,8,128]{2,0,1:T(8,128)(2,1)}, bf16[256,8,128]{2,0,1:T(8,128)(2,1)S(1)}, u32[]{:S(2)}) copy-start(bf16[256,8,128]{2,0,1:T(8,128)(2,1)S(1)} %convert_element_type.26) | copy-start | bytes 1572868 | tf_op jit(solution)/shard_map/while
  346.1 11.0 %collective-permute-start = (bf16[256,4,128]{2,0,1:T(8,128)(2,1)S(1)}, bf16[256,4,128]{2,0,1:T(8,128)(2,1)S(1)}, u32[]{:S(2)}, u32[]{:S(2)}) collective-permute-start(bf16[256,4,128]{2,0,1:T(8,128)(2,1)S(1)} %bitcast.92), channel_id=1, source_target_pairs={{4,0},{8,4},{12,8},{16,12},{20,16},{24,20},{28,24},{5,1},{9,5},{13... | collective-permute-start | bytes 786440 | tf_op jit(solution)/shard_map/while/body/eval_jaxpr/ppermute | solution.py:25
  348.0 14.8 %collective-permute-start.1 = (bf16[256,4,128]{2,0,1:T(8,128)(2,1)S(1)}, bf16[256,4,128]{2,0,1:T(8,128)(2,1)}, u32[]{:S(2)}, u32[]{:S(2)}) collective-permute-start(bf16[256,4,128]{2,0,1:T(8,128)(2,1)S(1)} %bitcast.93), channel_id=1, source_target_pairs={{0,4},{4,8},{8,12},{12,16},{16,20},{20,24},{24,28},{1,5},{5,9},{9,... | collective-permute-start | bytes 786440 | tf_op jit(solution)/shard_map/while/body/eval_jaxpr/ppermute | solution.py:25
  (4 other events, 35.3 us)
